TPU v7x, 32 devices: a whole 2x2x4 slice. The times are simulated.
32 devices in a mesh: gx: 8 (over y, x, core), gy: 4 (over z).
Axes of the slice: x: 2, y: 2, z: 4, core: 2. Of those that a mesh axis runs over, the one named last changes fastest.
Arguments:
- tracer_amounts: bfloat16 [2, 512, 512, 128], P(None, ('gx', 'gy')), may hold values from 0.099609375 to 3
- zonal_transit_ratio: float32 [2, 512, 512], P(None, 'gx', 'gy'), may hold values from -0.5 to 0.5
- meridional_transit_ratio: float32 [2, 512, 512], P(None, 'gx', 'gy'), may hold values from -0.45 to 0.45
- moisture_ratio: float32 [2, 512, 512], P(None, 'gx', 'gy'), may hold values from 0.2 to 0.9
- stratum_depths: float32 [2, 512, 512], P(None, 'gx', 'gy'), may hold values from 0.5 to 2
- sun_elevation_factor: float32 [512, 512], P('gx', 'gy'), may hold values from 0.2 to 1
- thermal_anomaly: float32 [2, 512, 512], P(None, 'gx', 'gy'), may hold values from -6 to 6
- particle_class_map: int32 [512, 512], P(('gx', 'gy')), may hold values from 0 to 7
- ground_cover_kind: int32 [512, 512], P(('gx', 'gy')), may hold values from 0 to 23
- arid_extinction_table: bfloat16 [128, 64], replicated, may hold values from 0 to 0.015625
- swelling_factors: bfloat16 [128, 64], replicated, may hold values from 0 to 0.00390625
- settling_velocities: float32 [24, 128], replicated, may hold values from 0.05 to 2
- arriving_irradiance: float32 [4], replicated, may hold values from 0.5 to 2
Outputs:
- updated_tracer_amounts: float32 [2, 512, 512, 128], P(None, ('gx', 'gy'))
- updated_thermal_anomaly: float32 [2, 512, 512], P(None, 'gx', 'gy')
All inputs are finite; a program needn't handle non-finite values.
Results may differ from a plain program's by a relative error of at most 0.00075.
Values may be sent and summed in bfloat16 or wider, within the bound.
A program may use at most 128 MiB of HBM per device.

v0:
```python
import jax
import jax.numpy as jnp
from jax import lax
from jax.sharding import PartitionSpec as P

SUB = 3
NBIN = 8
NW = 4
SPREAD_FACTOR = 0.2


def padded(cells, sides, width):
    for axis, dim in sides:
        count = lax.axis_size(axis)
        ends = count - 1
        head = lax.slice_in_dim(cells, 0, width, axis=dim)
        tail = lax.slice_in_dim(cells, cells.shape[dim] - width, cells.shape[dim], axis=dim)
        cells = jnp.concatenate(
            [
                lax.ppermute(tail, axis, [(i, (i + 1) % count) for i in range(ends)]),
                cells,
                lax.ppermute(head, axis, [((i + 1) % count, i) for i in range(ends)]),
            ],
            axis=dim,
        )
    return cells


def upwind(tracer, west_side, east_side, south_side, north_side, east_courant, north_courant):
    return (
        tracer
        - jnp.maximum(east_courant, 0.0) * (tracer - west_side)
        - jnp.minimum(east_courant, 0.0) * (east_side - tracer)
        - jnp.maximum(north_courant, 0.0) * (tracer - south_side)
        - jnp.minimum(north_courant, 0.0) * (north_side - tracer)
    )


def advance(widened, east_courant, north_courant):
    inner = widened[:, 1:-1]
    padded_y = jnp.pad(inner, ((0, 0), (0, 0), (1, 1), (0, 0)))
    return upwind(
        inner,
        widened[:, :-2],
        widened[:, 2:],
        padded_y[:, :, :-2],
        padded_y[:, :, 2:],
        east_courant,
        north_courant,
    )


def radiate(optical, cosine, sunlight):
    layers_count = optical.shape[0]
    wavelengths = optical.shape[1] // 2
    weights = sunlight.reshape((wavelengths,) + (1,) * (optical.ndim - 2))
    overhead = jnp.zeros_like(optical[0, :wavelengths])
    layers = [None] * layers_count
    for height in reversed(range(layers_count)):
        transmitted = jnp.exp(-overhead / cosine)
        layers[height] = cosine * jnp.sum(
            weights * optical[height, wavelengths:] * transmitted, axis=0
        )
        overhead = overhead + optical[height, :wavelengths]
    return jnp.stack(layers)


def per_device(
    tracer_amounts,
    zonal_transit_ratio,
    meridional_transit_ratio,
    moisture_ratio,
    stratum_depths,
    sun_elevation_factor,
    thermal_anomaly,
    particle_class_map,
    ground_cover_kind,
    arid_extinction_table,
    swelling_factors,
    settling_velocities,
    arriving_irradiance,
):
    tier_pile = thermal_anomaly.shape[0]
    strip_width = tracer_amounts.shape[1]
    species_count = tracer_amounts.shape[3]
    warmed_fringe_points = padded(
        thermal_anomaly.astype(jnp.bfloat16), (("gx", 1), ("gy", 2)), 1
    ).astype(thermal_anomaly.dtype)
    second_difference_map = (
        warmed_fringe_points[:, 2:, 1:-1]
        + warmed_fringe_points[:, :-2, 1:-1]
        + warmed_fringe_points[:, 1:-1, 2:]
        + warmed_fringe_points[:, 1:-1, :-2]
        - 4.0 * thermal_anomaly
    )
    fields = jnp.concatenate(
        [zonal_transit_ratio, meridional_transit_ratio, moisture_ratio, stratum_depths], axis=0
    )
    relayed = lax.all_to_all(fields, "gy", split_axis=1, concat_axis=2, tiled=True)
    moisture = relayed[2 * tier_pile : 3 * tier_pile]
    layer_depth = relayed[3 * tier_pile : 4 * tier_pile]
    widened = padded(tracer_amounts, ((("gx", "gy"), 1),), SUB).astype(jnp.float32)
    wind_rims = padded(relayed[: 2 * tier_pile], ((("gx", "gy"), 1),), SUB)
    span_width = strip_width + 2 * SUB
    first_column = lax.axis_index(("gx", "gy")) * strip_width - SUB
    grid_width = strip_width * lax.axis_size(("gx", "gy"))
    column_index = first_column + lax.iota(jnp.int32, span_width)
    inside = ((column_index >= 0) & (column_index < grid_width)).astype(jnp.float32)
    tracer = widened
    for substep in range(SUB):
        lower_edge = substep + 1
        upper_edge = span_width - substep - 1
        east_courant = wind_rims[:tier_pile, lower_edge:upper_edge][..., None]
        north_courant = wind_rims[tier_pile:, lower_edge:upper_edge][..., None]
        tracer = (
            advance(tracer, east_courant, north_courant)
            * inside[lower_edge:upper_edge][None, :, None, None]
        )
    land_count = settling_velocities.shape[0]
    one_hot = (ground_cover_kind[..., None] == lax.iota(jnp.int32, land_count)).astype(jnp.float32)
    loss_rate = jnp.dot(
        one_hot.reshape(-1, land_count), settling_velocities, precision=lax.Precision.HIGHEST
    ).reshape(strip_width, -1, species_count)
    loss_rate = loss_rate / layer_depth[0][..., None]
    updated_tracer_amounts = jnp.concatenate(
        [(tracer[0] / (1.0 + loss_rate))[None], tracer[1:]], axis=0
    )
    rounded = updated_tracer_amounts.astype(jnp.bfloat16)
    optics_table = jnp.concatenate([arid_extinction_table, swelling_factors], axis=1)
    projected = jnp.einsum(
        "lxys,sq->lqxy", rounded, optics_table, preferred_element_type=jnp.float32
    )
    projected = projected.reshape(tier_pile, 2, NBIN, 2 * NW, strip_width, -1)
    growth = moisture / (1.0 - moisture)
    combined = projected[:, 0] + growth[:, None, None] * projected[:, 1]
    bin_mask = (particle_class_map[None] == lax.iota(jnp.int32, NBIN)[:, None, None]).astype(
        jnp.float32
    )
    optical = jnp.sum(combined * bin_mask[None, :, None], axis=1) * layer_depth[:, None]
    payload = optical.reshape(tier_pile * 2 * NW, strip_width, -1)
    returned = lax.all_to_all(payload, "gy", split_axis=2, concat_axis=1, tiled=True)
    warming_tendency = radiate(
        returned.reshape(tier_pile, 2 * NW, returned.shape[1], returned.shape[2]),
        sun_elevation_factor,
        arriving_irradiance,
    )
    updated_thermal_anomaly = (
        thermal_anomaly + SPREAD_FACTOR * second_difference_map + warming_tendency
    )
    return (updated_tracer_amounts, updated_thermal_anomaly)


def solution(mesh):
    return jax.shard_map(
        per_device,
        mesh=mesh,
        in_specs=(
            P(None, ("gx", "gy"), None, None),
            P(None, "gx", "gy"),
            P(None, "gx", "gy"),
            P(None, "gx", "gy"),
            P(None, "gx", "gy"),
            P("gx", "gy"),
            P(None, "gx", "gy"),
            P(("gx", "gy"), None),
            P(("gx", "gy"), None),
            P(),
            P(),
            P(),
            P(),
        ),
        out_specs=(P(None, ("gx", "gy"), None, None), P(None, "gx", "gy")),
        check_vma=False,
    )
```

profile of v0, /device:TPU:3, one launch (start us, length us, event | category | flops | bytes accessed | tf_op | source)
XLA Modules:
  0.0 168.0 jit_solution(12056350276605661121)
XLA Ops:
  0.6 0.9 copy.36
  1.5 0.9 copy.37
  2.4 0.9 copy.38
  3.3 0.9 copy.39
  4.2 0.8 pad_maximum_fusion.1
  5.1 4.6 %all-to-all-start = ((f32[8,64,128]{2,0,1:T(8,128)}), f32[8,64,128]{2,0,1:T(8,128)S(1)}, u32[]{:S(2)}, u32[]{:S(2)}) async-start(f32[8,64,128]{2,0,1:T(8,128)} %pad_maximum_fusion.1), calls=%async_computation | async-start | bytes 524288 | tf_op jit(solution)/shard_map/all_to_all | solution.py:99
  9.7 2.4 %fusion.48 = (bf16[2,3,512,128]{3,2,1,0:T(8,128)(2,1)}, bf16[2,3,512,128]{3,2,1,0:T(8,128)(2,1)S(1)}) fusion(bf16[2,16,512,128]{3,2,1,0:T(8,128)(2,1)} %param.13), kind=kLoop, calls=%fused_computation.92 | loop fusion | bytes 3145728 | tf_op jit(solution)/shard_map/slice | solution.py:17
  12.0 3.4 %collective-permute-start = (bf16[2,3,512,128]{3,2,1,0:T(8,128)(2,1)}, bf16[2,3,512,128]{3,2,1,0:T(8,128)(2,1)S(1)}, u32[]{:S(2)}, u32[]{:S(2)}) collective-permute-start(bf16[2,3,512,128]{3,2,1,0:T(8,128)(2,1)} %get-tuple-element.4), channel_id=1, source_target_pairs={{0,1},{1,2},{2,3},{3,4},{4,5},{5,6},{6,7},{7,8},{8,9},{9,10},{10,1... | collective-permute-start | bytes 2359304 | tf_op jit(solution)/shard_map/ppermute | solution.py:20
  15.4 4.8 %collective-permute-start.1 = (bf16[2,3,512,128]{3,2,1,0:T(8,128)(2,1)S(1)}, bf16[2,3,512,128]{3,2,1,0:T(8,128)(2,1)S(1)}, u32[]{:S(2)}, u32[]{:S(2)}) collective-permute-start(bf16[2,3,512,128]{3,2,1,0:T(8,128)(2,1)S(1)} %get-tuple-element.5), channel_id=1, source_target_pairs={{1,0},{2,1},{3,2},{4,3},{5,4},{6,5},{7,6},{8,7},{9,8},{10,9},{11,1... | collective-permute-start | bytes 2359304 | tf_op jit(solution)/shard_map/ppermute | solution.py:22
  20.5 0.8 convert_element_type.31
  21.3 0.8 fusion.30
  22.3 0.7 fusion.49
  23.7 1.9 %collective-permute-start.2 = (f32[4,3,512]{2,1,0:T(4,128)}, f32[4,3,512]{2,1,0:T(4,128)S(1)}, u32[]{:S(2)}, u32[]{:S(2)}) collective-permute-start(f32[4,3,512]{2,1,0:T(4,128)} %get-tuple-element.20), channel_id=1, source_target_pairs={{0,1},{1,2},{2,3},{3,4},{4,5},{5,6},{6,7},{7,8},{8,9},{9,10},{10,1... | collective-permute-start | bytes 73736 | tf_op jit(solution)/shard_map/ppermute | solution.py:20
  25.6 5.4 %collective-permute-start.3 = (f32[4,3,512]{2,1,0:T(4,128)}, f32[4,3,512]{2,1,0:T(4,128)S(1)}, u32[]{:S(2)}, u32[]{:S(2)}) collective-permute-start(f32[4,3,512]{2,1,0:T(4,128)} %get-tuple-element.21), channel_id=1, source_target_pairs={{1,0},{2,1},{3,2},{4,3},{5,4},{6,5},{7,6},{8,7},{9,8},{10,9},{11,1... | collective-permute-start | bytes 73736 | tf_op jit(solution)/shard_map/ppermute | solution.py:22
  31.0 0.9 slice.197
  32.6 1.5 max.43
  34.0 0.6 max.45
  35.3 0.7 min.45
  36.0 0.7 mul.235
  36.6 17.5 %collective-permute-done.2 = f32[4,3,512]{2,1,0:T(4,128)S(1)} collective-permute-done((f32[4,3,512]{2,1,0:T(4,128)}, f32[4,3,512]{2,1,0:T(4,128)S(1)}, u32[]{:S(2)}, u32[]{:S(2)}) %collective-permute-start.2) | collective-permute-done | bytes 24608 | tf_op jit(solution)/shard_map/ppermute | solution.py:20
  54.1 0.8 collective-permute-done.3
  55.0 0.7 slice_maximum_fusion.3
  55.7 0.7 slice_maximum_fusion.1
  56.4 3.5 %maximum_convert_fusion = f32[2,22,512,128]{3,2,1,0:T(8,128)S(1)} fusion(bf16[2,3,512,128]{3,2,1,0:T(8,128)(2,1)S(1)} %collective-permute-done.1, bf16[2,16,512,128]{3,2,1,0:T(8,128)(2,1)} %param.13, bf16[2,3,512,128]{3,2,1,0:T(8,128)(2,1)S(1)} %collective-permute-done), kind=kLoop, calls=%fused_computation.28 | loop fusion | flops 8650752 | bytes 17301504 | tf_op jit(solution)/shard_map/convert_element_type | solution.py:102
  60.0 4.7 %slice.203 = f32[2,20,512,128]{3,2,1,0:T(8,128)} slice(f32[2,22,512,128]{3,2,1,0:T(8,128)S(1)} %maximum_convert_fusion), slice={[0:2], [1:21], [0:512], [0:128]} | slice | bytes 20971520 | tf_op jit(solution)/shard_map/slice | solution.py:40
  64.7 15.3 %fusion.4 = f32[2,20,512,128]{3,2,1,0:T(8,128)} fusion(f32[2,20,512,128]{3,2,1,0:T(8,128)} %slice.203, f32[2,22,512,128]{3,2,1,0:T(8,128)S(1)} %maximum_convert_fusion, f32[20]{0:T(128)S(1)} %slice.167, f32[2,20,512]{2,1,0:T(8,128)S(1)} %copy-done.3, f32[2,20,512]{2,1,0:T(8,128)S(1)} %copy-done.4, f32[2,20,512]{2,1,0:T(8,128)S(1)} %get-tuple-element.17, ...), kind=kLoop, calls=%fused_computation.5 | loop fusion | flops 34078720 | bytes 42270800 | tf_op jit(solution)/shard_map/mul | solution.py:116
  80.1 3.7 %slice-done = f32[2,18,512,128]{3,2,1,0:T(8,128)S(1)} async-done(((f32[2,20,512,128]{3,2,1,0:T(8,128)}), f32[2,18,512,128]{3,2,1,0:T(8,128)S(1)}, s32[]{:S(2)}) %slice-start) | async-done | bytes 9437208 | tf_op jit(solution)/shard_map/slice | solution.py:40
  83.7 13.3 %fusion.11 = f32[2,18,512,128]{3,2,1,0:T(8,128)S(1)} fusion(f32[2,18,512,128]{3,2,1,0:T(8,128)S(1)} %slice-done, f32[2,20,512,128]{3,2,1,0:T(8,128)} %fusion.4, f32[18]{0:T(128)S(1)} %slice.175, f32[2,18,512]{2,1,0:T(8,128)} %get-tuple-element.14, f32[2,18,512]{2,1,0:T(8,128)} %get-tuple-element.15, f32[2,18,512]{2,1,0:T(8,128)S(1)} %get-tuple-element.13, ...), kind=kLoop, calls=%fused_computation.14 | loop fusion | flops 30670848 | bytes 38043720 | tf_op jit(solution)/shard_map/mul | solution.py:116
  97.9 10.9 %fusion.18 = f32[2,16,512,128]{3,2,1,0:T(8,128)} fusion(f32[2,16,512,128]{3,2,1,0:T(8,128)S(1)} %slice.216, f32[2,18,512,128]{3,2,1,0:T(8,128)S(1)} %fusion.11, f32[16]{0:T(128)S(1)} %slice.183, f32[2,16,512]{2,1,0:T(8,128)S(1)} %copy-done.10, f32[2,16,512]{2,1,0:T(8,128)S(1)} %copy-done.8, f32[2,16,512]{2,1,0:T(8,128)S(1)} %copy-done.9, ...), kind=kLoop, calls=%fused_computation.23 | loop fusion | flops 27262976 | bytes 33816640 | tf_op jit(solution)/shard_map/mul | solution.py:116
  108.8 3.4 %copy-done.2 = f32[2,16,512,128]{3,2,1,0:T(8,128)S(1)} copy-done((f32[2,16,512,128]{3,2,1,0:T(8,128)S(1)}, f32[2,16,512,128]{3,2,1,0:T(8,128)}, u32[]{:S(2)}) %copy-start.2) | copy-done | bytes 8388632
  112.2 6.7 %fusion.26 = f32[1,16,512,128]{3,2,1,0:T(8,128)} fusion(f32[2,16,512,128]{3,2,1,0:T(8,128)S(1)} %copy-done.2, f32[16,512]{1,0:T(8,128)S(1)} %bitcast.93, s32[16,512]{1,0:T(8,128)} %param.21, f32[24,128]{1,0:T(8,128)S(1)} %copy-done), kind=kOutput, calls=%fused_computation.37 | convolution fusion | flops 305332224 | bytes 8466432 | tf_op jit(solution)/shard_map/dot_general | solution.py:121
  118.9 3.5 %pad_maximum_fusion = f32[2,16,512,128]{3,2,1,0:T(8,128)S(1)} fusion(f32[1,16,512,128]{3,2,1,0:T(8,128)S(1)} %slice-done.1, f32[1,16,512,128]{3,2,1,0:T(8,128)} %fusion.26), kind=kLoop, calls=%fused_computation.27 | loop fusion | flops 2097152 | bytes 16777216 | tf_op jit(solution)/shard_map/concatenate | solution.py:125
  122.4 1.3 fusion.27
  123.7 2.1 %copy-done.1 = f32[2,16,512,128]{3,2,1,0:T(8,128)} copy-done((f32[2,16,512,128]{3,2,1,0:T(8,128)}, f32[2,16,512,128]{3,2,1,0:T(8,128)S(1)}, u32[]{:S(2)}) %copy-start.1) | copy-done | bytes 8388632
  125.8 1.4 fusion.24
  127.6 3.6 %copy.44 = f32[16,16,512]{1,0,2:T(8,128)} copy(f32[16,16,512]{2,1,0:T(8,128)S(1)} %bitcast.85) | data formatting | bytes 1048576 | tf_op jit(solution)/shard_map/mul | solution.py:139
  131.2 4.6 %reshape.118 = f32[4,1,32768]{2,1,0:T(1,128)} reshape(f32[512,16,16]{2,1,0:T(8,128)} %bitcast.83) | data formatting | bytes 1048576
  135.9 3.5 %all-to-all-start.1 = ((f32[4,1,32768]{2,1,0:T(1,128)}), f32[4,1,32768]{2,1,0:T(1,128)S(1)}, u32[]{:S(2)}, u32[]{:S(2)}) async-start(f32[4,1,32768]{2,1,0:T(1,128)} %reshape.118), calls=%async_computation.1 | async-start | bytes 1048576 | tf_op jit(solution)/shard_map/all_to_all | solution.py:141
  139.4 4.2 %collective-permute-start.4 = (bf16[2,1,128]{2,1,0:T(2,128)(2,1)S(1)}, bf16[2,1,128]{2,1,0:T(2,128)(2,1)S(1)}, u32[]{:S(2)}, u32[]{:S(2)}) collective-permute-start(bf16[2,1,128]{2,1,0:T(2,128)(2,1)S(1)} %get-tuple-element.26), channel_id=1, source_target_pairs={{0,4},{4,8},{8,12},{12,16},{16,20},{20,24},{24,28},{1,5},{5,9},{9,... | collective-permute-start | bytes 1544 | tf_op jit(solution)/shard_map/ppermute | solution.py:20
  143.5 2.1 %collective-permute-start.5 = (bf16[2,1,128]{2,1,0:T(2,128)(2,1)S(1)}, bf16[2,1,128]{2,1,0:T(2,128)(2,1)S(1)}, u32[]{:S(2)}, u32[]{:S(2)}) collective-permute-start(bf16[2,1,128]{2,1,0:T(2,128)(2,1)S(1)} %get-tuple-element.27), channel_id=1, source_target_pairs={{4,0},{8,4},{12,8},{16,12},{20,16},{24,20},{28,24},{5,1},{9,5},{13... | collective-permute-start | bytes 1544 | tf_op jit(solution)/shard_map/ppermute | solution.py:22
  145.7 3.7 %collective-permute-done.5 = bf16[2,1,128]{2,1,0:T(2,128)(2,1)S(1)} collective-permute-done((bf16[2,1,128]{2,1,0:T(2,128)(2,1)S(1)}, bf16[2,1,128]{2,1,0:T(2,128)(2,1)S(1)}, u32[]{:S(2)}, u32[]{:S(2)}) %collective-permute-start.5) | collective-permute-done | bytes 544 | tf_op jit(solution)/shard_map/ppermute | solution.py:22
  149.4 3.9 %collective-permute-start.6 = (bf16[2,66,1]{2,1,0:T(8,128)(2,1)S(1)}, bf16[2,66,1]{2,1,0:T(8,128)(2,1)S(1)}, u32[]{:S(2)}, u32[]{:S(2)}) collective-permute-start(bf16[2,66,1]{2,1,0:T(8,128)(2,1)S(1)} %get-tuple-element.22), channel_id=1, source_target_pairs={{0,1},{1,2},{2,3},{4,5},{5,6},{6,7},{8,9},{9,10},{10,11},{12,13},{... | collective-permute-start | bytes 800 | tf_op jit(solution)/shard_map/ppermute | solution.py:20
  153.3 1.3 collective-permute-start.7
  154.7 3.4 %collective-permute-done.7 = bf16[2,66,1]{2,1,0:T(8,128)(2,1)S(1)} collective-permute-done((bf16[2,66,1]{2,1,0:T(8,128)(2,1)S(1)}, bf16[2,66,1]{2,1,0:T(8,128)(2,1)S(1)}, u32[]{:S(2)}, u32[]{:S(2)}) %collective-permute-start.7) | collective-permute-done | bytes 296 | tf_op jit(solution)/shard_map/ppermute | solution.py:22
  158.7 2.2 %reduce = f32[4,32768]{1,0:T(4,128)S(1)} reduce(f32[4,1,32768]{2,1,0:T(1,128)S(1)} %all-to-all-done.1, f32[]{:T(128)} %broadcast.108), dimensions={1}, to_apply=%all_to_all.25.reduce_sub_computation | reduce | bytes 1048580 | tf_op jit(solution)/shard_map/all_to_all | solution.py:141
  160.8 3.4 %reshape.119 = f32[512,16,16]{2,1,0:T(8,128)} reshape(f32[4,32768]{1,0:T(4,128)S(1)} %reduce) | data formatting | bytes 1048576
  164.3 2.8 %copy.48 = f32[16,16,4,128]{3,2,1,0:T(4,128)S(1)} copy(f32[16,16,4,128]{1,0,3,2:T(8,128)} %bitcast.84) | data formatting | bytes 1048576 | tf_op jit(solution)/shard_map/all_to_all | solution.py:141
  167.3 0.8 fusion.43
  (64 shorter events, 4.6 us)
Async XLA Ops:
  0.6 108.2 %copy-start = (f32[24,128]{1,0:T(8,128)S(1)}, f32[24,128]{1,0:T(8,128)}, u32[]{:S(2)}) copy-start(f32[24,128]{1,0:T(8,128)} %param.24) | copy-start | bytes 36868
  5.1 17.0 %all-to-all-start = ((f32[8,64,128]{2,0,1:T(8,128)}), f32[8,64,128]{2,0,1:T(8,128)S(1)}, u32[]{:S(2)}, u32[]{:S(2)}) async-start(f32[8,64,128]{2,0,1:T(8,128)} %pad_maximum_fusion.1), calls=%async_computation | async-start | bytes 524288 | tf_op jit(solution)/shard_map/all_to_all | solution.py:99
  12.0 44.4 %collective-permute-start = (bf16[2,3,512,128]{3,2,1,0:T(8,128)(2,1)}, bf16[2,3,512,128]{3,2,1,0:T(8,128)(2,1)S(1)}, u32[]{:S(2)}, u32[]{:S(2)}) collective-permute-start(bf16[2,3,512,128]{3,2,1,0:T(8,128)(2,1)} %get-tuple-element.4), channel_id=1, source_target_pairs={{0,1},{1,2},{2,3},{3,4},{4,5},{5,6},{6,7},{7,8},{8,9},{9,10},{10,1... | collective-permute-start | bytes 2359304 | tf_op jit(solution)/shard_map/ppermute | solution.py:20
  15.4 41.1 %collective-permute-start.1 = (bf16[2,3,512,128]{3,2,1,0:T(8,128)(2,1)S(1)}, bf16[2,3,512,128]{3,2,1,0:T(8,128)(2,1)S(1)}, u32[]{:S(2)}, u32[]{:S(2)}) collective-permute-start(bf16[2,3,512,128]{3,2,1,0:T(8,128)(2,1)S(1)} %get-tuple-element.5), channel_id=1, source_target_pairs={{1,0},{2,1},{3,2},{4,3},{5,4},{6,5},{7,6},{8,7},{9,8},{10,9},{11,1... | collective-permute-start | bytes 2359304 | tf_op jit(solution)/shard_map/ppermute | solution.py:22
  23.7 30.5 %collective-permute-start.2 = (f32[4,3,512]{2,1,0:T(4,128)}, f32[4,3,512]{2,1,0:T(4,128)S(1)}, u32[]{:S(2)}, u32[]{:S(2)}) collective-permute-start(f32[4,3,512]{2,1,0:T(4,128)} %get-tuple-element.20), channel_id=1, source_target_pairs={{0,1},{1,2},{2,3},{3,4},{4,5},{5,6},{6,7},{7,8},{8,9},{9,10},{10,1... | collective-permute-start | bytes 73736 | tf_op jit(solution)/shard_map/ppermute | solution.py:20
  25.6 29.3 %collective-permute-start.3 = (f32[4,3,512]{2,1,0:T(4,128)}, f32[4,3,512]{2,1,0:T(4,128)S(1)}, u32[]{:S(2)}, u32[]{:S(2)}) collective-permute-start(f32[4,3,512]{2,1,0:T(4,128)} %get-tuple-element.21), channel_id=1, source_target_pairs={{1,0},{2,1},{3,2},{4,3},{5,4},{6,5},{7,6},{8,7},{9,8},{10,9},{11,1... | collective-permute-start | bytes 73736 | tf_op jit(solution)/shard_map/ppermute | solution.py:22
  60.0 4.7 %copy-start.3 = (f32[2,20,512]{2,1,0:T(8,128)S(1)}, f32[2,20,512]{2,1,0:T(8,128)}, u32[]{:S(2)}) copy-start(f32[2,20,512]{2,1,0:T(8,128)} %get-tuple-element.18) | copy-start | bytes 245764
  60.0 4.7 %copy-start.4 = (f32[2,20,512]{2,1,0:T(8,128)S(1)}, f32[2,20,512]{2,1,0:T(8,128)}, u32[]{:S(2)}) copy-start(f32[2,20,512]{2,1,0:T(8,128)} %get-tuple-element.19) | copy-start | bytes 245764
  80.0 3.7 %slice-start = ((f32[2,20,512,128]{3,2,1,0:T(8,128)}), f32[2,18,512,128]{3,2,1,0:T(8,128)S(1)}, s32[]{:S(2)}) async-start(f32[2,20,512,128]{3,2,1,0:T(8,128)} %fusion.4), calls=%async_computation.2 | async-start | bytes 18874368 | tf_op jit(solution)/shard_map/slice | solution.py:40
  97.0 0.8 copy-start.7
  97.0 0.9 copy-start.8
  97.0 0.9 copy-start.9
  97.0 0.9 copy-start.10
  108.8 3.4 %copy-start.2 = (f32[2,16,512,128]{3,2,1,0:T(8,128)S(1)}, f32[2,16,512,128]{3,2,1,0:T(8,128)}, u32[]{:S(2)}) copy-start(f32[2,16,512,128]{3,2,1,0:T(8,128)} %fusion.18) | copy-start | bytes 25165828
  112.2 6.7 %slice-start.1 = ((f32[2,16,512,128]{3,2,1,0:T(8,128)}), f32[1,16,512,128]{3,2,1,0:T(8,128)S(1)}, s32[]{:S(2)}) async-start(f32[2,16,512,128]{3,2,1,0:T(8,128)} %fusion.18), calls=%async_computation.3 | async-start | bytes 8388608 | tf_op jit(solution)/shard_map/slice | solution.py:126
  118.9 3.5 %copy-start.13 = (bf16[128,64]{0,1:T(8,128)(2,1)S(1)}, bf16[128,64]{0,1:T(8,128)(2,1)}, u32[]{:S(2)}) copy-start(bf16[128,64]{0,1:T(8,128)(2,1)} %param.23) | copy-start | bytes 49156
  118.9 3.5 %copy-start.14 = (bf16[128,64]{0,1:T(8,128)(2,1)S(1)}, bf16[128,64]{0,1:T(8,128)(2,1)}, u32[]{:S(2)}) copy-start(bf16[128,64]{0,1:T(8,128)(2,1)} %param.22) | copy-start | bytes 49156
  122.4 3.4 %copy-start.1 = (f32[2,16,512,128]{3,2,1,0:T(8,128)}, f32[2,16,512,128]{3,2,1,0:T(8,128)S(1)}, u32[]{:S(2)}) copy-start(f32[2,16,512,128]{3,2,1,0:T(8,128)S(1)} %pad_maximum_fusion) | copy-start | bytes 25165828
  122.4 3.4 %copy-start.6 = (f32[2,16,512]{2,1,0:T(8,128)S(1)}, f32[2,16,512]{2,1,0:T(8,128)}, u32[]{:S(2)}) copy-start(f32[2,16,512]{2,1,0:T(8,128)} %subtract_divide_fusion) | copy-start | bytes 196612
  125.8 1.4 copy-start.12
  127.2 27.4 %copy-start.5 = (f32[64,128]{1,0:T(8,128)S(1)}, f32[64,128]{1,0:T(8,128)}, u32[]{:S(2)}) copy-start(f32[64,128]{1,0:T(8,128)} %param.18) | copy-start | bytes 98308
  131.2 35.9 %copy-start.15 = (f32[4]{0:T(128)S(1)}, f32[4]{0:T(128)}, u32[]{:S(2)}) copy-start(f32[4]{0:T(128)} %param.25) | copy-start | bytes 52
  131.2 36.0 %copy-start.11 = (f32[2,64,128]{2,1,0:T(8,128)S(1)}, f32[2,64,128]{2,1,0:T(8,128)}, u32[]{:S(2)}) copy-start(f32[2,64,128]{2,1,0:T(8,128)} %param.19) | copy-start | bytes 196612
  135.9 22.3 %all-to-all-start.1 = ((f32[4,1,32768]{2,1,0:T(1,128)}), f32[4,1,32768]{2,1,0:T(1,128)S(1)}, u32[]{:S(2)}, u32[]{:S(2)}) async-start(f32[4,1,32768]{2,1,0:T(1,128)} %reshape.118), calls=%async_computation.1 | async-start | bytes 1048576 | tf_op jit(solution)/shard_map/all_to_all | solution.py:141
  139.4 6.3 %collective-permute-start.4 = (bf16[2,1,128]{2,1,0:T(2,128)(2,1)S(1)}, bf16[2,1,128]{2,1,0:T(2,128)(2,1)S(1)}, u32[]{:S(2)}, u32[]{:S(2)}) collective-permute-start(bf16[2,1,128]{2,1,0:T(2,128)(2,1)S(1)} %get-tuple-element.26), channel_id=1, source_target_pairs={{0,4},{4,8},{8,12},{12,16},{16,20},{20,24},{24,28},{1,5},{5,9},{9,... | collective-permute-start | bytes 1544 | tf_op jit(solution)/shard_map/ppermute | solution.py:20
  143.5 5.8 %collective-permute-start.5 = (bf16[2,1,128]{2,1,0:T(2,128)(2,1)S(1)}, bf16[2,1,128]{2,1,0:T(2,128)(2,1)S(1)}, u32[]{:S(2)}, u32[]{:S(2)}) collective-permute-start(bf16[2,1,128]{2,1,0:T(2,128)(2,1)S(1)} %get-tuple-element.27), channel_id=1, source_target_pairs={{4,0},{8,4},{12,8},{16,12},{20,16},{24,20},{28,24},{5,1},{9,5},{13... | collective-permute-start | bytes 1544 | tf_op jit(solution)/shard_map/ppermute | solution.py:22
  149.4 5.2 %collective-permute-start.6 = (bf16[2,66,1]{2,1,0:T(8,128)(2,1)S(1)}, bf16[2,66,1]{2,1,0:T(8,128)(2,1)S(1)}, u32[]{:S(2)}, u32[]{:S(2)}) collective-permute-start(bf16[2,66,1]{2,1,0:T(8,128)(2,1)S(1)} %get-tuple-element.22), channel_id=1, source_target_pairs={{0,1},{1,2},{2,3},{4,5},{5,6},{6,7},{8,9},{9,10},{10,11},{12,13},{... | collective-permute-start | bytes 800 | tf_op jit(solution)/shard_map/ppermute | solution.py:20
  153.3 4.7 %collective-permute-start.7 = (bf16[2,66,1]{2,1,0:T(8,128)(2,1)S(1)}, bf16[2,66,1]{2,1,0:T(8,128)(2,1)S(1)}, u32[]{:S(2)}, u32[]{:S(2)}) collective-permute-start(bf16[2,66,1]{2,1,0:T(8,128)(2,1)S(1)} %get-tuple-element.23), channel_id=1, source_target_pairs={{1,0},{2,1},{3,2},{5,4},{6,5},{7,6},{9,8},{10,9},{11,10},{13,12},{... | collective-permute-start | bytes 800 | tf_op jit(solution)/shard_map/ppermute | solution.py:22
where the time goes:
time: 169 us; the launch traced here: 168 us
  other arithmetic  56.4 us (33%)
  local copies, waits for them, and re-layouts  42.3 us (25%)
  starting transfers between devices  35 us (21%)
  waiting for transfers between devices  25.3 us (15%)
  matrix products  7.92 us (5%)
    mul x3, other arithmetic, per_device(): advance(tracer, east_courant, north_courant)  39.5 us
    unnamed x39, local copies, waits for them, and re-layouts  17.5 us
    ppermute x4, waiting for transfers between devices, padded(): lax.ppermute(tail, axis, [(i, (i + 1) % count) for i in range(ends)])  17.5 us
    ppermute x4, starting transfers between devices, padded(): lax.ppermute(head, axis, [((i + 1) % count, i) for i in range(ends)])  13.7 us
    ppermute x4, starting transfers between devices, padded(): lax.ppermute(tail, axis, [(i, (i + 1) % count) for i in range(ends)])  13.3 us
    slice x4, local copies, waits for them, and re-layouts, advance(): inner = widened[:, 1:-1]  8.95 us
    ppermute x4, waiting for transfers between devices, padded(): lax.ppermute(head, axis, [((i + 1) % count, i) for i in range(ends)])  7.83 us
    dot_general x1, matrix products, per_device(): jnp.dot(one_hot.reshape(-1, land_count), settling_velocities, precision=l...  6.66 us
  transfers between devices with their start and end apart: 10, of which 4 were waited for; matrix products, arithmetic and copies ran while one was open for 8% of the time, Pallas kernels for 0%

commit v1 on v0

--- a/solution.py
+++ b/solution.py
@@ -138,7 +138,10 @@
     )
     optical = jnp.sum(combined * bin_mask[None, :, None], axis=1) * layer_depth[:, None]
     payload = optical.reshape(tier_pile * 2 * NW, strip_width, -1)
-    returned = lax.all_to_all(payload, "gy", split_axis=2, concat_axis=1, tiled=True)
+    returned = jnp.concatenate(
+        lax.all_to_all(jnp.stack(jnp.split(payload, lax.axis_size("gy"), axis=2)), "gy", 0, 0),
+        axis=1,
+    )
     warming_tendency = radiate(
         returned.reshape(tier_pile, 2 * NW, returned.shape[1], returned.shape[2]),
         sun_elevation_factor,

time: 169 us -> 153 us (0.905)
  local copies, waits for them, and re-layouts: 42.3 us -> 27.3 us
    unnamed x39 -> x37, local copies, waits for them, and re-layouts: 17.5 us -> 9.46 us
    mul x3 -> x2, local copies, waits for them, and re-layouts: 4.58 us -> 0.96 us  [per_device(): jnp.sum(combined * bin_mask[None, :, None], axis=1) * layer_depth[:, None]]
    all_to_all x3 -> x1, local copies, waits for them, and re-layouts: 3.37 us -> 0.04 us  [per_device(): lax.all_to_all(jnp.stack(jnp.split(payload, lax.axis_size('gy'), axis=2))...]
    all_to_all x1 -> x0, other arithmetic: 2.17 us -> none  [per_device(): lax.all_to_all(payload, 'gy', split_axis=2, concat_axis=1, tiled=True)]
  transfers between devices with their start and end apart: 10 -> 10, of which waited for: 4 -> 4; matrix products, arithmetic and copies ran while one was open for 8% -> 9% of each run, Pallas kernels for 0% -> 0%
where the time goes in v1:
time: 153 us; the launch traced here: 152 us
  other arithmetic  55.1 us (36%)
  starting transfers between devices  34.9 us (23%)
  local copies, waits for them, and re-layouts  27.3 us (18%)
  waiting for transfers between devices  25.5 us (17%)
  matrix products  7.91 us (5%)
    mul x3, other arithmetic, per_device(): advance(tracer, east_courant, north_courant)  39.5 us
    ppermute x4, waiting for transfers between devices, padded(): lax.ppermute(tail, axis, [(i, (i + 1) % count) for i in range(ends)])  17.5 us
    ppermute x4, starting transfers between devices, padded(): lax.ppermute(head, axis, [((i + 1) % count, i) for i in range(ends)])  13.5 us
    ppermute x4, starting transfers between devices, padded(): lax.ppermute(tail, axis, [(i, (i + 1) % count) for i in range(ends)])  13.3 us
    unnamed x37, local copies, waits for them, and re-layouts  9.46 us
    slice x4, local copies, waits for them, and re-layouts, advance(): inner = widened[:, 1:-1]  8.95 us
    ppermute x4, waiting for transfers between devices, padded(): lax.ppermute(head, axis, [((i + 1) % count, i) for i in range(ends)])  8.01 us
    dot_general x1, matrix products, per_device(): jnp.dot(one_hot.reshape(-1, land_count), settling_velocities, precision=l...  6.65 us
  transfers between devices with their start and end apart: 10, of which 4 were waited for; matrix products, arithmetic and copies ran while one was open for 9% of the time, Pallas kernels for 0%

profile of v1, /device:TPU:3, one launch (start us, length us, event | category | flops | bytes accessed | tf_op | source)
XLA Modules:
  0.0 151.7 jit_solution(5787807966658939250)
XLA Ops:
  0.6 0.9 copy.37
  1.5 0.9 copy.38
  2.4 0.9 copy.39
  3.3 0.9 copy.40
  4.2 0.8 pad_maximum_fusion.2
  5.0 4.6 %all-to-all-start = ((f32[8,64,128]{2,0,1:T(8,128)}), f32[8,64,128]{2,0,1:T(8,128)S(1)}, u32[]{:S(2)}, u32[]{:S(2)}) async-start(f32[8,64,128]{2,0,1:T(8,128)} %pad_maximum_fusion.2), calls=%async_computation | async-start | bytes 524288 | tf_op jit(solution)/shard_map/all_to_all | solution.py:99
  9.6 2.4 %fusion.48 = (bf16[2,3,512,128]{3,2,1,0:T(8,128)(2,1)}, bf16[2,3,512,128]{3,2,1,0:T(8,128)(2,1)S(1)}) fusion(bf16[2,16,512,128]{3,2,1,0:T(8,128)(2,1)} %param.13), kind=kLoop, calls=%fused_computation.97 | loop fusion | bytes 3145728 | tf_op jit(solution)/shard_map/slice | solution.py:17
  12.0 3.4 %collective-permute-start = (bf16[2,3,512,128]{3,2,1,0:T(8,128)(2,1)}, bf16[2,3,512,128]{3,2,1,0:T(8,128)(2,1)S(1)}, u32[]{:S(2)}, u32[]{:S(2)}) collective-permute-start(bf16[2,3,512,128]{3,2,1,0:T(8,128)(2,1)} %get-tuple-element.4), channel_id=1, source_target_pairs={{0,1},{1,2},{2,3},{3,4},{4,5},{5,6},{6,7},{7,8},{8,9},{9,10},{10,1... | collective-permute-start | bytes 2359304 | tf_op jit(solution)/shard_map/ppermute | solution.py:20
  15.4 4.8 %collective-permute-start.1 = (bf16[2,3,512,128]{3,2,1,0:T(8,128)(2,1)S(1)}, bf16[2,3,512,128]{3,2,1,0:T(8,128)(2,1)S(1)}, u32[]{:S(2)}, u32[]{:S(2)}) collective-permute-start(bf16[2,3,512,128]{3,2,1,0:T(8,128)(2,1)S(1)} %get-tuple-element.5), channel_id=1, source_target_pairs={{1,0},{2,1},{3,2},{4,3},{5,4},{6,5},{7,6},{8,7},{9,8},{10,9},{11,1... | collective-permute-start | bytes 2359304 | tf_op jit(solution)/shard_map/ppermute | solution.py:22
  20.4 0.8 convert_element_type.31
  21.3 0.8 fusion.30
  22.3 0.7 fusion.49
  23.0 0.6 fusion.50
  23.7 1.9 %collective-permute-start.2 = (f32[4,3,512]{2,1,0:T(4,128)}, f32[4,3,512]{2,1,0:T(4,128)S(1)}, u32[]{:S(2)}, u32[]{:S(2)}) collective-permute-start(f32[4,3,512]{2,1,0:T(4,128)} %get-tuple-element.24), channel_id=1, source_target_pairs={{0,1},{1,2},{2,3},{3,4},{4,5},{5,6},{6,7},{7,8},{8,9},{9,10},{10,1... | collective-permute-start | bytes 73736 | tf_op jit(solution)/shard_map/ppermute | solution.py:20
  25.6 5.4 %collective-permute-start.3 = (f32[4,3,512]{2,1,0:T(4,128)}, f32[4,3,512]{2,1,0:T(4,128)S(1)}, u32[]{:S(2)}, u32[]{:S(2)}) collective-permute-start(f32[4,3,512]{2,1,0:T(4,128)} %get-tuple-element.25), channel_id=1, source_target_pairs={{1,0},{2,1},{3,2},{4,3},{5,4},{6,5},{7,6},{8,7},{9,8},{10,9},{11,1... | collective-permute-start | bytes 73736 | tf_op jit(solution)/shard_map/ppermute | solution.py:22
  31.0 0.9 slice.197
  31.9 0.6 subtract_divide_fusion
  32.6 1.5 max.43
  34.0 0.6 max.45
  34.7 0.6 min.43
  35.3 0.7 min.45
  36.0 0.7 mul.235
  36.6 17.5 %collective-permute-done.2 = f32[4,3,512]{2,1,0:T(4,128)S(1)} collective-permute-done((f32[4,3,512]{2,1,0:T(4,128)}, f32[4,3,512]{2,1,0:T(4,128)S(1)}, u32[]{:S(2)}, u32[]{:S(2)}) %collective-permute-start.2) | collective-permute-done | bytes 24608 | tf_op jit(solution)/shard_map/ppermute | solution.py:20
  54.1 0.8 collective-permute-done.3
  55.0 0.7 slice_maximum_fusion.3
  55.7 0.7 slice_maximum_fusion.1
  56.4 3.5 %maximum_convert_fusion = f32[2,22,512,128]{3,2,1,0:T(8,128)S(1)} fusion(bf16[2,3,512,128]{3,2,1,0:T(8,128)(2,1)S(1)} %collective-permute-done.1, bf16[2,16,512,128]{3,2,1,0:T(8,128)(2,1)} %param.13, bf16[2,3,512,128]{3,2,1,0:T(8,128)(2,1)S(1)} %collective-permute-done), kind=kLoop, calls=%fused_computation.28 | loop fusion | flops 8650752 | bytes 17301504 | tf_op jit(solution)/shard_map/convert_element_type | solution.py:102
  59.9 4.7 %slice.203 = f32[2,20,512,128]{3,2,1,0:T(8,128)} slice(f32[2,22,512,128]{3,2,1,0:T(8,128)S(1)} %maximum_convert_fusion), slice={[0:2], [1:21], [0:512], [0:128]} | slice | bytes 20971520 | tf_op jit(solution)/shard_map/slice | solution.py:40
  64.7 15.4 %fusion.4 = f32[2,20,512,128]{3,2,1,0:T(8,128)} fusion(f32[2,20,512,128]{3,2,1,0:T(8,128)} %slice.203, f32[2,22,512,128]{3,2,1,0:T(8,128)S(1)} %maximum_convert_fusion, f32[20]{0:T(128)S(1)} %slice.167, f32[2,20,512]{2,1,0:T(8,128)S(1)} %copy-done.3, f32[2,20,512]{2,1,0:T(8,128)S(1)} %copy-done.4, f32[2,20,512]{2,1,0:T(8,128)S(1)} %get-tuple-element.21, ...), kind=kLoop, calls=%fused_computation.5 | loop fusion | flops 34078720 | bytes 42270800 | tf_op jit(solution)/shard_map/mul | solution.py:116
  80.1 3.7 %slice-done = f32[2,18,512,128]{3,2,1,0:T(8,128)S(1)} async-done(((f32[2,20,512,128]{3,2,1,0:T(8,128)}), f32[2,18,512,128]{3,2,1,0:T(8,128)S(1)}, s32[]{:S(2)}) %slice-start) | async-done | bytes 9437208 | tf_op jit(solution)/shard_map/slice | solution.py:40
  83.7 13.3 %fusion.11 = f32[2,18,512,128]{3,2,1,0:T(8,128)S(1)} fusion(f32[2,18,512,128]{3,2,1,0:T(8,128)S(1)} %slice-done, f32[2,20,512,128]{3,2,1,0:T(8,128)} %fusion.4, f32[18]{0:T(128)S(1)} %slice.175, f32[2,18,512]{2,1,0:T(8,128)} %get-tuple-element.18, f32[2,18,512]{2,1,0:T(8,128)} %get-tuple-element.19, f32[2,18,512]{2,1,0:T(8,128)S(1)} %get-tuple-element.17, ...), kind=kLoop, calls=%fused_computation.14 | loop fusion | flops 30670848 | bytes 38043720 | tf_op jit(solution)/shard_map/mul | solution.py:116
  97.0 0.6 slice.216
  97.9 10.9 %fusion.18 = f32[2,16,512,128]{3,2,1,0:T(8,128)} fusion(f32[2,16,512,128]{3,2,1,0:T(8,128)S(1)} %slice.216, f32[2,18,512,128]{3,2,1,0:T(8,128)S(1)} %fusion.11, f32[16]{0:T(128)S(1)} %slice.183, f32[2,16,512]{2,1,0:T(8,128)S(1)} %copy-done.10, f32[2,16,512]{2,1,0:T(8,128)S(1)} %copy-done.8, f32[2,16,512]{2,1,0:T(8,128)S(1)} %copy-done.9, ...), kind=kLoop, calls=%fused_computation.23 | loop fusion | flops 27262976 | bytes 33816640 | tf_op jit(solution)/shard_map/mul | solution.py:116
  108.8 3.4 %copy-done.2 = f32[2,16,512,128]{3,2,1,0:T(8,128)S(1)} copy-done((f32[2,16,512,128]{3,2,1,0:T(8,128)S(1)}, f32[2,16,512,128]{3,2,1,0:T(8,128)}, u32[]{:S(2)}) %copy-start.2) | copy-done | bytes 8388632
  112.2 6.6 %fusion.26 = f32[1,16,512,128]{3,2,1,0:T(8,128)} fusion(f32[2,16,512,128]{3,2,1,0:T(8,128)S(1)} %copy-done.2, f32[16,512]{1,0:T(8,128)S(1)} %bitcast.96, s32[16,512]{1,0:T(8,128)} %param.21, f32[24,128]{1,0:T(8,128)S(1)} %copy-done), kind=kOutput, calls=%fused_computation.37 | convolution fusion | flops 305332224 | bytes 8466432 | tf_op jit(solution)/shard_map/dot_general | solution.py:121
  118.9 3.5 %pad_maximum_fusion = f32[2,16,512,128]{3,2,1,0:T(8,128)S(1)} fusion(f32[1,16,512,128]{3,2,1,0:T(8,128)S(1)} %slice-done.1, f32[1,16,512,128]{3,2,1,0:T(8,128)} %fusion.26), kind=kLoop, calls=%fused_computation.27 | loop fusion | flops 2097152 | bytes 16777216 | tf_op jit(solution)/shard_map/concatenate | solution.py:125
  122.4 1.3 fusion.27
  123.7 2.1 %copy-done.1 = f32[2,16,512,128]{3,2,1,0:T(8,128)} copy-done((f32[2,16,512,128]{3,2,1,0:T(8,128)}, f32[2,16,512,128]{3,2,1,0:T(8,128)S(1)}, u32[]{:S(2)}) %copy-start.1) | copy-done | bytes 8388632
  125.8 1.4 fusion.24
  127.7 0.8 pad_maximum_fusion.1
  128.5 3.5 %all-to-all-start.1 = ((f32[4,16,16,128]{3,2,1,0:T(8,128)}), f32[4,16,16,128]{3,2,1,0:T(8,128)S(1)}, u32[]{:S(2)}, u32[]{:S(2)}) async-start(f32[4,16,16,128]{3,2,1,0:T(8,128)} %pad_maximum_fusion.1), calls=%async_computation.1 | async-start | bytes 1048576 | tf_op jit(solution)/shard_map/all_to_all | solution.py:142
  132.0 4.2 %collective-permute-start.4 = (bf16[2,1,128]{2,1,0:T(2,128)(2,1)S(1)}, bf16[2,1,128]{2,1,0:T(2,128)(2,1)S(1)}, u32[]{:S(2)}, u32[]{:S(2)}) collective-permute-start(bf16[2,1,128]{2,1,0:T(2,128)(2,1)S(1)} %get-tuple-element.30), channel_id=1, source_target_pairs={{0,4},{4,8},{8,12},{12,16},{16,20},{20,24},{24,28},{1,5},{5,9},{9,... | collective-permute-start | bytes 1544 | tf_op jit(solution)/shard_map/ppermute | solution.py:20
  136.2 1.9 %collective-permute-start.5 = (bf16[2,1,128]{2,1,0:T(2,128)(2,1)S(1)}, bf16[2,1,128]{2,1,0:T(2,128)(2,1)S(1)}, u32[]{:S(2)}, u32[]{:S(2)}) collective-permute-start(bf16[2,1,128]{2,1,0:T(2,128)(2,1)S(1)} %get-tuple-element.31), channel_id=1, source_target_pairs={{4,0},{8,4},{12,8},{16,12},{20,16},{24,20},{28,24},{5,1},{9,5},{13... | collective-permute-start | bytes 1544 | tf_op jit(solution)/shard_map/ppermute | solution.py:22
  138.1 3.9 %collective-permute-done.5 = bf16[2,1,128]{2,1,0:T(2,128)(2,1)S(1)} collective-permute-done((bf16[2,1,128]{2,1,0:T(2,128)(2,1)S(1)}, bf16[2,1,128]{2,1,0:T(2,128)(2,1)S(1)}, u32[]{:S(2)}, u32[]{:S(2)}) %collective-permute-start.5) | collective-permute-done | bytes 544 | tf_op jit(solution)/shard_map/ppermute | solution.py:22
  142.1 3.9 %collective-permute-start.6 = (bf16[2,66,1]{2,1,0:T(8,128)(2,1)S(1)}, bf16[2,66,1]{2,1,0:T(8,128)(2,1)S(1)}, u32[]{:S(2)}, u32[]{:S(2)}) collective-permute-start(bf16[2,66,1]{2,1,0:T(8,128)(2,1)S(1)} %get-tuple-element.26), channel_id=1, source_target_pairs={{0,1},{1,2},{2,3},{4,5},{5,6},{6,7},{8,9},{9,10},{10,11},{12,13},{... | collective-permute-start | bytes 800 | tf_op jit(solution)/shard_map/ppermute | solution.py:20
  145.9 1.3 collective-permute-start.7
  147.3 3.4 %collective-permute-done.7 = bf16[2,66,1]{2,1,0:T(8,128)(2,1)S(1)} collective-permute-done((bf16[2,66,1]{2,1,0:T(8,128)(2,1)S(1)}, bf16[2,66,1]{2,1,0:T(8,128)(2,1)S(1)}, u32[]{:S(2)}, u32[]{:S(2)}) %collective-permute-start.7) | collective-permute-done | bytes 296 | tf_op jit(solution)/shard_map/ppermute | solution.py:22
  151.0 0.8 fusion.43
  (60 shorter events, 1.7 us)
Async XLA Ops:
  0.6 108.2 %copy-start = (f32[24,128]{1,0:T(8,128)S(1)}, f32[24,128]{1,0:T(8,128)}, u32[]{:S(2)}) copy-start(f32[24,128]{1,0:T(8,128)} %param.24) | copy-start | bytes 36868
  5.0 17.0 %all-to-all-start = ((f32[8,64,128]{2,0,1:T(8,128)}), f32[8,64,128]{2,0,1:T(8,128)S(1)}, u32[]{:S(2)}, u32[]{:S(2)}) async-start(f32[8,64,128]{2,0,1:T(8,128)} %pad_maximum_fusion.2), calls=%async_computation | async-start | bytes 524288 | tf_op jit(solution)/shard_map/all_to_all | solution.py:99
  12.0 44.4 %collective-permute-start = (bf16[2,3,512,128]{3,2,1,0:T(8,128)(2,1)}, bf16[2,3,512,128]{3,2,1,0:T(8,128)(2,1)S(1)}, u32[]{:S(2)}, u32[]{:S(2)}) collective-permute-start(bf16[2,3,512,128]{3,2,1,0:T(8,128)(2,1)} %get-tuple-element.4), channel_id=1, source_target_pairs={{0,1},{1,2},{2,3},{3,4},{4,5},{5,6},{6,7},{7,8},{8,9},{9,10},{10,1... | collective-permute-start | bytes 2359304 | tf_op jit(solution)/shard_map/ppermute | solution.py:20
  15.4 41.0 %collective-permute-start.1 = (bf16[2,3,512,128]{3,2,1,0:T(8,128)(2,1)S(1)}, bf16[2,3,512,128]{3,2,1,0:T(8,128)(2,1)S(1)}, u32[]{:S(2)}, u32[]{:S(2)}) collective-permute-start(bf16[2,3,512,128]{3,2,1,0:T(8,128)(2,1)S(1)} %get-tuple-element.5), channel_id=1, source_target_pairs={{1,0},{2,1},{3,2},{4,3},{5,4},{6,5},{7,6},{8,7},{9,8},{10,9},{11,1... | collective-permute-start | bytes 2359304 | tf_op jit(solution)/shard_map/ppermute | solution.py:22
  23.7 30.4 %collective-permute-start.2 = (f32[4,3,512]{2,1,0:T(4,128)}, f32[4,3,512]{2,1,0:T(4,128)S(1)}, u32[]{:S(2)}, u32[]{:S(2)}) collective-permute-start(f32[4,3,512]{2,1,0:T(4,128)} %get-tuple-element.24), channel_id=1, source_target_pairs={{0,1},{1,2},{2,3},{3,4},{4,5},{5,6},{6,7},{7,8},{8,9},{9,10},{10,1... | collective-permute-start | bytes 73736 | tf_op jit(solution)/shard_map/ppermute | solution.py:20
  25.6 29.3 %collective-permute-start.3 = (f32[4,3,512]{2,1,0:T(4,128)}, f32[4,3,512]{2,1,0:T(4,128)S(1)}, u32[]{:S(2)}, u32[]{:S(2)}) collective-permute-start(f32[4,3,512]{2,1,0:T(4,128)} %get-tuple-element.25), channel_id=1, source_target_pairs={{1,0},{2,1},{3,2},{4,3},{5,4},{6,5},{7,6},{8,7},{9,8},{10,9},{11,1... | collective-permute-start | bytes 73736 | tf_op jit(solution)/shard_map/ppermute | solution.py:22
  59.9 4.7 %copy-start.3 = (f32[2,20,512]{2,1,0:T(8,128)S(1)}, f32[2,20,512]{2,1,0:T(8,128)}, u32[]{:S(2)}) copy-start(f32[2,20,512]{2,1,0:T(8,128)} %get-tuple-element.22) | copy-start | bytes 245764
  59.9 4.7 %copy-start.4 = (f32[2,20,512]{2,1,0:T(8,128)S(1)}, f32[2,20,512]{2,1,0:T(8,128)}, u32[]{:S(2)}) copy-start(f32[2,20,512]{2,1,0:T(8,128)} %get-tuple-element.23) | copy-start | bytes 245764
  80.0 3.7 %slice-start = ((f32[2,20,512,128]{3,2,1,0:T(8,128)}), f32[2,18,512,128]{3,2,1,0:T(8,128)S(1)}, s32[]{:S(2)}) async-start(f32[2,20,512,128]{3,2,1,0:T(8,128)} %fusion.4), calls=%async_computation.2 | async-start | bytes 18874368 | tf_op jit(solution)/shard_map/slice | solution.py:40
  97.0 0.8 copy-start.7
  97.0 0.9 copy-start.8
  97.0 0.9 copy-start.9
  97.0 0.9 copy-start.10
  108.8 3.4 %copy-start.2 = (f32[2,16,512,128]{3,2,1,0:T(8,128)S(1)}, f32[2,16,512,128]{3,2,1,0:T(8,128)}, u32[]{:S(2)}) copy-start(f32[2,16,512,128]{3,2,1,0:T(8,128)} %fusion.18) | copy-start | bytes 25165828
  112.2 6.7 %slice-start.1 = ((f32[2,16,512,128]{3,2,1,0:T(8,128)}), f32[1,16,512,128]{3,2,1,0:T(8,128)S(1)}, s32[]{:S(2)}) async-start(f32[2,16,512,128]{3,2,1,0:T(8,128)} %fusion.18), calls=%async_computation.3 | async-start | bytes 8388608 | tf_op jit(solution)/shard_map/slice | solution.py:126
  118.9 3.5 %copy-start.13 = (bf16[128,64]{0,1:T(8,128)(2,1)S(1)}, bf16[128,64]{0,1:T(8,128)(2,1)}, u32[]{:S(2)}) copy-start(bf16[128,64]{0,1:T(8,128)(2,1)} %param.23) | copy-start | bytes 49156
  118.9 3.5 %copy-start.14 = (bf16[128,64]{0,1:T(8,128)(2,1)S(1)}, bf16[128,64]{0,1:T(8,128)(2,1)}, u32[]{:S(2)}) copy-start(bf16[128,64]{0,1:T(8,128)(2,1)} %param.22) | copy-start | bytes 49156
  122.4 3.4 %copy-start.1 = (f32[2,16,512,128]{3,2,1,0:T(8,128)}, f32[2,16,512,128]{3,2,1,0:T(8,128)S(1)}, u32[]{:S(2)}) copy-start(f32[2,16,512,128]{3,2,1,0:T(8,128)S(1)} %pad_maximum_fusion) | copy-start | bytes 25165828
  122.4 3.4 %copy-start.6 = (f32[2,16,512]{2,1,0:T(8,128)S(1)}, f32[2,16,512]{2,1,0:T(8,128)}, u32[]{:S(2)}) copy-start(f32[2,16,512]{2,1,0:T(8,128)} %subtract_divide_fusion) | copy-start | bytes 196612
  125.8 1.4 copy-start.12
  125.8 21.5 %copy-start.5 = (f32[64,128]{1,0:T(8,128)S(1)}, f32[64,128]{1,0:T(8,128)}, u32[]{:S(2)}) copy-start(f32[64,128]{1,0:T(8,128)} %param.18) | copy-start | bytes 98308
  125.8 25.1 %copy-start.15 = (f32[4]{0:T(128)S(1)}, f32[4]{0:T(128)}, u32[]{:S(2)}) copy-start(f32[4]{0:T(128)} %param.25) | copy-start | bytes 52
  125.8 25.2 %copy-start.11 = (f32[2,64,128]{2,1,0:T(8,128)S(1)}, f32[2,64,128]{2,1,0:T(8,128)}, u32[]{:S(2)}) copy-start(f32[2,64,128]{2,1,0:T(8,128)} %param.19) | copy-start | bytes 196612
  128.5 22.3 %all-to-all-start.1 = ((f32[4,16,16,128]{3,2,1,0:T(8,128)}), f32[4,16,16,128]{3,2,1,0:T(8,128)S(1)}, u32[]{:S(2)}, u32[]{:S(2)}) async-start(f32[4,16,16,128]{3,2,1,0:T(8,128)} %pad_maximum_fusion.1), calls=%async_computation.1 | async-start | bytes 1048576 | tf_op jit(solution)/shard_map/all_to_all | solution.py:142
  132.0 6.1 %collective-permute-start.4 = (bf16[2,1,128]{2,1,0:T(2,128)(2,1)S(1)}, bf16[2,1,128]{2,1,0:T(2,128)(2,1)S(1)}, u32[]{:S(2)}, u32[]{:S(2)}) collective-permute-start(bf16[2,1,128]{2,1,0:T(2,128)(2,1)S(1)} %get-tuple-element.30), channel_id=1, source_target_pairs={{0,4},{4,8},{8,12},{12,16},{16,20},{20,24},{24,28},{1,5},{5,9},{9,... | collective-permute-start | bytes 1544 | tf_op jit(solution)/shard_map/ppermute | solution.py:20
  136.2 5.8 %collective-permute-start.5 = (bf16[2,1,128]{2,1,0:T(2,128)(2,1)S(1)}, bf16[2,1,128]{2,1,0:T(2,128)(2,1)S(1)}, u32[]{:S(2)}, u32[]{:S(2)}) collective-permute-start(bf16[2,1,128]{2,1,0:T(2,128)(2,1)S(1)} %get-tuple-element.31), channel_id=1, source_target_pairs={{4,0},{8,4},{12,8},{16,12},{20,16},{24,20},{28,24},{5,1},{9,5},{13... | collective-permute-start | bytes 1544 | tf_op jit(solution)/shard_map/ppermute | solution.py:22
  142.1 5.2 %collective-permute-start.6 = (bf16[2,66,1]{2,1,0:T(8,128)(2,1)S(1)}, bf16[2,66,1]{2,1,0:T(8,128)(2,1)S(1)}, u32[]{:S(2)}, u32[]{:S(2)}) collective-permute-start(bf16[2,66,1]{2,1,0:T(8,128)(2,1)S(1)} %get-tuple-element.26), channel_id=1, source_target_pairs={{0,1},{1,2},{2,3},{4,5},{5,6},{6,7},{8,9},{9,10},{10,11},{12,13},{... | collective-permute-start | bytes 800 | tf_op jit(solution)/shard_map/ppermute | solution.py:20
  145.9 4.7 %collective-permute-start.7 = (bf16[2,66,1]{2,1,0:T(8,128)(2,1)S(1)}, bf16[2,66,1]{2,1,0:T(8,128)(2,1)S(1)}, u32[]{:S(2)}, u32[]{:S(2)}) collective-permute-start(bf16[2,66,1]{2,1,0:T(8,128)(2,1)S(1)} %get-tuple-element.27), channel_id=1, source_target_pairs={{1,0},{2,1},{3,2},{5,4},{6,5},{7,6},{9,8},{10,9},{11,10},{13,12},{... | collective-permute-start | bytes 800 | tf_op jit(solution)/shard_map/ppermute | solution.py:22
